TPU v7x, 512 devices: a whole 4x8x8 slice. The times are simulated.
512 devices in a mesh: seq: 32 (over x, z), tp: 16 (over y, core).
Axes of the slice: x: 4, y: 8, z: 8, core: 2. Of those that a mesh axis runs over, the one named last changes fastest.
Arguments:
- residual: bfloat16 [6144, 8192], P('seq', 'tp'), may hold values from -6 to 6
- attention: bfloat16 [1536, 8192], P('seq'), may hold values from -6 to 6
- quantized_codes: int32 [8192, 8192], P('seq', 'tp'), may hold values from 0 to 15
- absmax: float32 [8192, 128], P('seq', 'tp'), may hold values from 0.005 to 0.05
- adapter_down: bfloat16 [8192, 64], P('seq'), may hold values from -0.0625 to 0.0625
- adapter_up: bfloat16 [64, 8192], P(None, 'tp'), may hold values from -0.75 to 0.75
- routed_slot_gate: float32 [1536], P('seq'), may hold values from 0.2 to 1
- selected: int32 [1536], P('seq'), may hold values from 0 to 191, as said below
- counts: int32 [32], P('seq'), may hold values from 1 to 48, 768 in all
- cotangent: bfloat16 [6144, 8192], P('seq', 'tp'), may hold values from -0.59765625 to 0.59765625
Outputs:
- outgoing_residual: bfloat16 [6144, 8192], P('seq', 'tp')
- attention_output_grad: bfloat16 [1536, 8192], P(None, 'seq')
- adapter_down_gradient: float32 [8192, 64], P('seq')
- adapter_up_gradient: float32 [64, 8192], P(None, 'tp')
- router_gate_gradient: float32 [1536], P('seq')
Inputs may be any that keep to these rules, and one draw needn't show every extreme that they name: `counts`: every shard has at least one live slot, all shards together have 768, and some shard has all 48 slots live. `selected`: within each shard's 48 slots the entries are distinct token positions of that shard; only the first counts entries of a shard are live.
All inputs are finite; a program needn't handle non-finite values.
Results may differ from a plain program's by a relative error of at most 0.0058.
Values may be sent and summed in bfloat16 or wider, within the bound.
A program may use at most 64 MiB of HBM per device.

v0:
```python
import jax
import jax.numpy as jnp
from jax import lax
from jax.sharding import PartitionSpec as P

LEVELS = (
    -1.0,
    -0.6961928009986877,
    -0.5250730514526367,
    -0.39491748809814453,
    -0.28444138169288635,
    -0.18477343022823334,
    -0.09105003625154495,
    0.0,
    0.07958029955625534,
    0.16093020141124725,
    0.24611230194568634,
    0.33791524171829224,
    0.44070982933044434,
    0.5626170039176941,
    0.7229568362236023,
    1.0,
)
adapter_scale = 0.25


def precise_matmul(left, right):
    return jnp.dot(left, right, precision=lax.Precision.HIGHEST, preferred_element_type=jnp.float32)


def dequantize(quantized_codes, absmax):
    quantile_levels = jnp.zeros(quantized_codes.shape, jnp.float32)
    for level_code in range(16):
        quantile_levels = quantile_levels + jnp.where(
            quantized_codes == level_code, LEVELS[level_code], 0.0
        )
    block_size = quantized_codes.shape[1] // absmax.shape[1]
    scales = jnp.repeat(absmax, block_size, axis=1)
    return (quantile_levels * scales).astype(jnp.bfloat16)


def body(
    residual,
    attention,
    quantized_codes,
    absmax,
    adapter_down,
    adapter_up,
    routed_slot_gate,
    selected,
    counts,
    cotangent,
):
    projection_weight = dequantize(quantized_codes, absmax)
    adapter_up_single32 = adapter_up.astype(jnp.float32)
    home_slots = attention.shape[0]
    live_slot = jnp.arange(home_slots, dtype=jnp.int32) < counts[0]
    target = jnp.where(live_slot, selected, residual.shape[0])
    full_w, full_a = (
        lax.all_gather(projection_weight, "seq", axis=0, tiled=True),
        lax.all_gather(adapter_down, "seq", axis=0, tiled=True),
    )
    adapter_product = jnp.dot(attention, full_a, preferred_element_type=jnp.float32)
    block_output = jnp.dot(
        attention, full_w, preferred_element_type=jnp.float32
    ) + adapter_scale * precise_matmul(adapter_product, adapter_up_single32)
    picked = residual[selected].astype(jnp.float32)
    updated = (picked + routed_slot_gate[:, None] * block_output).astype(jnp.bfloat16)
    outgoing_residual = residual.at[target].set(updated, mode="drop")
    upstream = jnp.where(live_slot[:, None], cotangent[selected].astype(jnp.float32), 0.0)
    gate_part = jnp.sum(upstream * block_output, axis=1)
    output_gradient = (routed_slot_gate[:, None] * upstream).astype(jnp.bfloat16)
    head_part = jnp.dot(output_gradient, full_w.T, preferred_element_type=jnp.float32)
    adapter_rank_piece = adapter_scale * jnp.dot(
        output_gradient, adapter_up.T, preferred_element_type=jnp.float32
    )
    head_full, rank_full, router_gate_gradient = lax.psum(
        (head_part, adapter_rank_piece, gate_part), "tp"
    )
    adapter_rank_gradient = rank_full.astype(jnp.bfloat16)
    home_grad = (
        head_full + jnp.dot(adapter_rank_gradient, full_a.T, preferred_element_type=jnp.float32)
    ).astype(jnp.bfloat16)
    attention_output_grad = lax.all_to_all(
        home_grad, "seq", split_axis=1, concat_axis=0, tiled=True
    )
    adapter_down_gradient = lax.psum_scatter(
        jnp.dot(attention.T, adapter_rank_gradient, preferred_element_type=jnp.float32),
        "seq",
        scatter_dimension=0,
        tiled=True,
    )
    up_factor_piece = adapter_scale * precise_matmul(
        adapter_product.T, output_gradient.astype(jnp.float32)
    )
    adapter_up_gradient = lax.psum(up_factor_piece, "seq")
    return (
        outgoing_residual,
        attention_output_grad,
        adapter_down_gradient,
        adapter_up_gradient,
        router_gate_gradient,
    )


def solution(mesh):
    return jax.shard_map(
        body,
        mesh=mesh,
        in_specs=(
            P("seq", "tp"),
            P("seq", None),
            P("seq", "tp"),
            P("seq", "tp"),
            P("seq", None),
            P(None, "tp"),
            P("seq"),
            P("seq"),
            P("seq"),
            P("seq", "tp"),
        ),
        out_specs=(P("seq", "tp"), P(None, "seq"), P("seq", None), P(None, "tp"), P("seq")),
        check_vma=False,
    )
```

profile of v0, /device:TPU:8, one launch (start us, length us, event | category | flops | bytes accessed | tf_op | source)
XLA Modules:
  0.0 714.8 jit_solution(8451295507987079360)
XLA Ops:
  7.2 0.0 all-gather.3.cloned.1.call-start
  7.3 1.3 copy.33
  8.6 2.2 fusion.2
  10.8 0.0 all-gather.5.cloned.1.call-start
  10.8 0.7 all-gather.5.cloned.1.call-update
  11.5 0.0 all-reduce.4.cloned.1.call-start
  12.3 0.7 gather_fusion
  13.0 113.0 %all-gather.3.cloned.1.call-done = bf16[8192,512]{0,1:T(8,128)(2,1)} async-done(((bf16[256,512]{0,1:T(8,128)(2,1)}), bf16[8192,512]{0,1:T(8,128)(2,1)}) %all-gather.3.cloned.1.call-update) | async-done | bytes 8388624 | tf_op jit(solution)/shard_map/all_gather | solution.py:60
  126.0 6.1 fusion.8
  132.1 0.0 all-reduce.4.cloned.1.call-update
  132.1 0.0 all-reduce.6.cloned.1.call-start
  132.2 0.2 convolution_multiply_fusion.2
  132.4 71.0 %all-gather.5.cloned.1.call-done = bf16[8192,64]{0,1:T(8,128)(2,1)} async-done(((bf16[256,64]{0,1:T(8,128)(2,1)}), bf16[8192,64]{0,1:T(8,128)(2,1)}) %all-gather.5.cloned.1.call-update) | async-done | bytes 1048592 | tf_op jit(solution)/shard_map/all_gather | solution.py:61
  203.4 1.6 fusion.9
  205.1 0.9 convolution_multiply_fusion
  206.0 0.0 all-reduce.6.cloned.1.call-update
  206.0 0.0 reduce-scatter.2.cloned.1.call-start
  206.1 6.0 convolution_bitcast_fusion.1
  212.1 0.3 multiply_reduce_fusion
  212.4 42.8 %all-reduce = (bf16[48,64]{1,0:T(8,128)(2,1)S(1)}, f32[48]{0:T(128)}) all-reduce(f32[48,64]{1,0:T(8,128)S(1)} %convolution_multiply_fusion.2, f32[48]{0:T(128)S(1)} %get-tuple-element.9), channel_id=1, replica_groups=mesh['seq'=32,'tp'=16] {'tp'}, use_global_device_ids=true, to_apply=%region_2.3 | all-reduce | flops 3120 | bytes 18816 | tf_op jit(solution)/shard_map/psum | solution.py:77
  255.2 1.8 convolution_bitcast_fusion
  257.0 0.0 reduce-scatter.2.cloned.1.call-update
  257.1 64.0 %all-reduce.4.cloned.1.call-done = f32[48,8192]{1,0:T(8,128)} async-done(((f32[48,8192]{1,0:T(8,128)}), f32[48,8192]{1,0:T(8,128)}) %all-reduce.4.cloned.1.call-update) | async-done | bytes 1572880 | tf_op jit(solution)/shard_map/psum | solution.py:77
  321.1 1.8 fusion
  322.9 0.9 copy.51
  323.8 9.3 %all-to-all-start = ((bf16[48,32,256]{2,0,1:T(8,128)(2,1)}), bf16[48,32,256]{2,0,1:T(8,128)(2,1)S(1)}, u32[]{:S(2)}, u32[]{:S(2)}) async-start(bf16[48,32,256]{2,0,1:T(8,128)(2,1)} %bitcast.28), calls=%async_computation | async-start | bytes 1572864 | tf_op jit(solution)/shard_map/all_to_all | solution.py:84
  333.1 1.2 scatter_custom_fusion
  334.3 23.0 %all-to-all-done = bf16[48,32,256]{2,0,1:T(8,128)(2,1)S(1)} async-done(((bf16[48,32,256]{2,0,1:T(8,128)(2,1)}), bf16[48,32,256]{2,0,1:T(8,128)(2,1)S(1)}, u32[]{:S(2)}, u32[]{:S(2)}) %all-to-all-start) | async-done | bytes 786464 | tf_op jit(solution)/shard_map/all_to_all | solution.py:84
  357.3 123.7 %all-reduce.6.cloned.1.call-done = f32[64,512]{1,0:T(8,128)} async-done(((f32[64,512]{1,0:T(8,128)}), f32[64,512]{1,0:T(8,128)}) %all-reduce.6.cloned.1.call-update) | async-done | bytes 131088 | tf_op jit(solution)/shard_map/psum | solution.py:96
  481.0 224.9 %reduce-scatter.2.cloned.1.call-done = f32[256,64]{0,1:T(8,128)} async-done(((f32[8192,64]{0,1:T(8,128)}), f32[256,64]{0,1:T(8,128)}) %reduce-scatter.2.cloned.1.call-update) | async-done | bytes 65552 | tf_op jit(solution)/shard_map/reduce_scatter | solution.py:87
  705.9 0.9 copy.59
  706.7 1.6 copy.60
  (20 shorter events, 0.1 us)
Async XLA Ops:
  7.2 196.3 %copy-start = (bf16[48,8192]{1,0:T(8,128)(2,1)S(1)}, bf16[48,8192]{1,0:T(8,128)(2,1)}, u32[]{:S(2)}) copy-start(bf16[48,8192]{1,0:T(8,128)(2,1)} %param.11) | copy-start | bytes 2359300
  7.2 5.1 copy-start.7
  7.2 5.1 copy-start.4
  7.2 118.8 %copy-start.6 = (f32[48]{0:T(128)S(1)}, f32[48]{0:T(128)}, u32[]{:S(2)}) copy-start(f32[48]{0:T(128)} %param.16) | copy-start | bytes 580
  7.2 118.8 %all-gather.3.cloned.1.call-start = ((), (), s32[]{:S(2)}) async-start(), calls=%async_computation.2 | async-start | bytes 8650752 | tf_op jit(solution)/shard_map/all_gather | solution.py:60
  10.8 192.6 %all-gather.5.cloned.1.call-start = ((), (), s32[]{:S(2)}) async-start(), calls=%async_computation.3 | async-start | bytes 1081344 | tf_op jit(solution)/shard_map/all_gather | solution.py:61
  11.5 309.5 %all-reduce.4.cloned.1.call-start = ((), (), s32[]{:S(2)}) async-start(), calls=%async_computation.4 | async-start | bytes 3145728 | tf_op jit(solution)/shard_map/psum | solution.py:77
  13.0 119.2 %copy-start.5 = (bf16[64,512]{1,0:T(8,128)(2,1)S(1)}, bf16[64,512]{1,0:T(8,128)(2,1)}, u32[]{:S(2)}) copy-start(bf16[64,512]{1,0:T(8,128)(2,1)} %param.15) | copy-start | bytes 196612
  132.1 348.8 %all-reduce.6.cloned.1.call-start = ((), (), s32[]{:S(2)}) async-start(), calls=%async_computation.6 | async-start | bytes 262144 | tf_op jit(solution)/shard_map/psum | solution.py:96
  206.0 499.8 %reduce-scatter.2.cloned.1.call-start = ((), (), s32[]{:S(2)}) async-start(), calls=%async_computation.5 | async-start | bytes 2162688 | tf_op jit(solution)/shard_map/reduce_scatter | solution.py:87
  255.2 65.8 %copy-start.1 = (bf16[8192,64]{0,1:T(8,128)(2,1)S(1)}, bf16[8192,64]{0,1:T(8,128)(2,1)}, u32[]{:S(2)}) copy-start(bf16[8192,64]{0,1:T(8,128)(2,1)} %all-gather.5.cloned.1.call-done) | copy-start | bytes 3145732
  322.8 10.2 %copy-start.3 = (bf16[192,512]{1,0:T(8,128)(2,1)S(1)}, bf16[192,512]{1,0:T(8,128)(2,1)}, u32[]{:S(2)}) copy-start(bf16[192,512]{1,0:T(8,128)(2,1)} %param.10) | copy-start | bytes 589828
  323.8 33.5 %all-to-all-start = ((bf16[48,32,256]{2,0,1:T(8,128)(2,1)}), bf16[48,32,256]{2,0,1:T(8,128)(2,1)S(1)}, u32[]{:S(2)}, u32[]{:S(2)}) async-start(bf16[48,32,256]{2,0,1:T(8,128)(2,1)} %bitcast.28), calls=%async_computation | async-start | bytes 1572864 | tf_op jit(solution)/shard_map/all_to_all | solution.py:84
  334.3 374.0 %copy-start.2 = (bf16[192,512]{1,0:T(8,128)(2,1)}, bf16[192,512]{1,0:T(8,128)(2,1)S(1)}, u32[]{:S(2)}) copy-start(bf16[192,512]{1,0:T(8,128)(2,1)S(1)} %scatter_custom_fusion) | copy-start | bytes 589828
Sparse Core Ops, SparseCore 0:
  11.7 114.2 all-gather.2
  129.0 74.3 all-gather.4
  205.8 115.2 all-reduce.3
  325.3 155.5 all-reduce.5
  485.8 220.0 reduce-scatter.1
where the time goes:
time: 715 us
  waiting for transfers between devices  620 us (87%)
  blocking collectives  42.8 us (6%)
  matrix products  18.8 us (3%)
  between operations  14.6 us (2%)
  starting transfers between devices  9.47 us (1%)
    reduce_scatter x1, waiting for transfers between devices, body(): lax.psum_scatter(jnp.dot(attention.T, adapter_rank_gradient, preferred_el...  225 us
    psum x1, waiting for transfers between devices, body(): adapter_up_gradient = lax.psum(up_factor_piece, 'seq')  124 us
    all_gather x1, waiting for transfers between devices, body(): lax.all_gather(projection_weight, 'seq', axis=0, tiled=True)  113 us
    all_gather x1, waiting for transfers between devices, body(): lax.all_gather(adapter_down, 'seq', axis=0, tiled=True)  71 us
    psum x1, waiting for transfers between devices, body(): lax.psum((head_part, adapter_rank_piece, gate_part), 'tp')  64 us
    psum x1, blocking collectives, body(): lax.psum((head_part, adapter_rank_piece, gate_part), 'tp')  42.8 us
    all_to_all x1, waiting for transfers between devices, body(): lax.all_to_all(home_grad, 'seq', split_axis=1, concat_axis=0, tiled=True)  23 us
  transfers between devices with their start and end apart: 6, of which 6 were waited for; matrix products, arithmetic and copies ran while one was open for 3% of the time, Pallas kernels for 0%

commit v1 on v0

--- a/solution.py
+++ b/solution.py
@@ -57,7 +57,10 @@
     live_slot = jnp.arange(home_slots, dtype=jnp.int32) < counts[0]
     target = jnp.where(live_slot, selected, residual.shape[0])
     full_w, full_a = (
-        lax.all_gather(projection_weight, "seq", axis=0, tiled=True),
+        jnp.concatenate(
+            lax.all_to_all(jnp.stack([projection_weight] * lax.axis_size("seq")), "seq", 0, 0),
+            axis=0,
+        ),
         lax.all_gather(adapter_down, "seq", axis=0, tiled=True),
     )
     adapter_product = jnp.dot(attention, full_a, preferred_element_type=jnp.float32)

time: 715 us -> 745 us (1.042)
  starting transfers between devices: 9.47 us -> 22.8 us
  waiting for transfers between devices: 620 us -> 629 us
    all_to_all x0 -> x1, waiting for transfers between devices: none -> 192 us  [body(): lax.all_to_all(jnp.stack([projection_weight] * lax.axis_size('seq')), 'se...]
    all_gather x1 -> x0, waiting for transfers between devices: 113 us -> none  [body(): lax.all_gather(projection_weight, 'seq', axis=0, tiled=True)]
    all_gather x1, waiting for transfers between devices: 71 us -> 0.02 us  [body(): lax.all_gather(adapter_down, 'seq', axis=0, tiled=True)]
    all_to_all x0 -> x1, starting transfers between devices: none -> 13.4 us  [body(): lax.all_to_all(jnp.stack([projection_weight] * lax.axis_size('seq')), 'se...]
  transfers between devices with their start and end apart: 6 -> 6, of which waited for: 6 -> 5; matrix products, arithmetic and copies ran while one was open for 3% -> 3% of each run, Pallas kernels for 0% -> 0%
where the time goes in v1:
time: 745 us
  waiting for transfers between devices  629 us (84%)
  blocking collectives  45.4 us (6%)
  starting transfers between devices  22.8 us (3%)
  matrix products  18.7 us (3%)
  between operations  16.5 us (2%)
  local copies, waits for them, and re-layouts  9.73 us (1%)
    reduce_scatter x1, waiting for transfers between devices, body(): lax.psum_scatter(jnp.dot(attention.T, adapter_rank_gradient, preferred_el...  225 us
    all_to_all x1, waiting for transfers between devices, body(): lax.all_to_all(jnp.stack([projection_weight] * lax.axis_size('seq')), 'se...  192 us
    psum x1, waiting for transfers between devices, body(): adapter_up_gradient = lax.psum(up_factor_piece, 'seq')  123 us
    psum x1, waiting for transfers between devices, body(): lax.psum((head_part, adapter_rank_piece, gate_part), 'tp')  64.8 us
    psum x1, blocking collectives, body(): lax.psum((head_part, adapter_rank_piece, gate_part), 'tp')  45.4 us
    all_to_all x1, waiting for transfers between devices, body(): lax.all_to_all(home_grad, 'seq', split_axis=1, concat_axis=0, tiled=True)  23.1 us
  transfers between devices with their start and end apart: 6, of which 5 were waited for; matrix products, arithmetic and copies ran while one was open for 3% of the time, Pallas kernels for 0%

profile of v1, /device:TPU:8, one launch (start us, length us, event | category | flops | bytes accessed | tf_op | source)
XLA Modules:
  0.0 744.6 jit_solution(6507905423675193379)
XLA Ops:
  8.0 1.3 copy.34
  9.3 1.5 fusion.2
  10.8 0.1 copy.49
  11.0 4.2 stack.2
  15.1 13.4 %all-to-all-start = ((bf16[32,256,512]{2,1,0:T(8,128)(2,1)}), bf16[32,256,512]{2,1,0:T(8,128)(2,1)}, u32[]{:S(2)}, u32[]{:S(2)}) async-start(bf16[32,256,512]{2,1,0:T(8,128)(2,1)} %stack.2), calls=%async_computation | async-start | bytes 16777216 | tf_op jit(solution)/shard_map/all_to_all | solution.py:61
  28.6 0.0 all-gather.2.cloned.1.call-start
  28.6 0.7 all-gather.2.cloned.1.call-update
  29.3 0.0 all-reduce.4.cloned.1.call-start
  30.1 0.7 gather_fusion
  30.8 191.6 %all-to-all-done = bf16[32,256,512]{2,1,0:T(8,128)(2,1)} async-done(((bf16[32,256,512]{2,1,0:T(8,128)(2,1)}), bf16[32,256,512]{2,1,0:T(8,128)(2,1)}, u32[]{:S(2)}, u32[]{:S(2)}) %all-to-all-start) | async-done | bytes 8388640 | tf_op jit(solution)/shard_map/all_to_all | solution.py:61
  222.3 7.1 fusion.8
  229.4 0.0 all-reduce.4.cloned.1.call-update
  229.4 0.0 all-reduce.6.cloned.1.call-start
  229.5 0.2 convolution_multiply_fusion.2
  229.7 0.0 all-gather.2.cloned.1.call-done
  229.7 1.6 fusion.9
  231.4 0.2 convolution_multiply_fusion.1
  231.5 0.9 convolution_multiply_fusion
  232.5 0.0 reduce-scatter.2.cloned.1.call-start
  232.6 5.1 multiply_reduce_fusion
  237.7 45.4 %all-reduce = (bf16[48,64]{1,0:T(8,128)(2,1)S(1)}, f32[48]{0:T(128)}) all-reduce(f32[48,64]{1,0:T(8,128)S(1)} %convolution_multiply_fusion.2, f32[48]{0:T(128)S(1)} %get-tuple-element.9), channel_id=1, replica_groups=mesh['seq'=32,'tp'=16] {'tp'}, use_global_device_ids=true, to_apply=%region_2.3 | all-reduce | flops 3120 | bytes 18816 | tf_op jit(solution)/shard_map/psum | solution.py:80
  283.1 1.8 convolution_bitcast_fusion
  284.9 64.8 %all-reduce.4.cloned.1.call-done = f32[48,8192]{1,0:T(8,128)} async-done(((f32[48,8192]{1,0:T(8,128)}), f32[48,8192]{1,0:T(8,128)}) %all-reduce.4.cloned.1.call-update) | async-done | bytes 1572880 | tf_op jit(solution)/shard_map/psum | solution.py:80
  349.7 1.8 fusion
  351.5 0.9 copy.53
  352.4 9.2 %all-to-all-start.1 = ((bf16[48,32,256]{2,0,1:T(8,128)(2,1)}), bf16[48,32,256]{2,0,1:T(8,128)(2,1)S(1)}, u32[]{:S(2)}, u32[]{:S(2)}) async-start(bf16[48,32,256]{2,0,1:T(8,128)(2,1)} %bitcast.31), calls=%async_computation.1 | async-start | bytes 1572864 | tf_op jit(solution)/shard_map/all_to_all | solution.py:87
  361.7 1.2 scatter_custom_fusion
  362.9 23.1 %all-to-all-done.1 = bf16[48,32,256]{2,0,1:T(8,128)(2,1)S(1)} async-done(((bf16[48,32,256]{2,0,1:T(8,128)(2,1)}), bf16[48,32,256]{2,0,1:T(8,128)(2,1)S(1)}, u32[]{:S(2)}, u32[]{:S(2)}) %all-to-all-start.1) | async-done | bytes 786464 | tf_op jit(solution)/shard_map/all_to_all | solution.py:87
  386.0 123.4 %all-reduce.6.cloned.1.call-done = f32[64,512]{1,0:T(8,128)} async-done(((f32[64,512]{1,0:T(8,128)}), f32[64,512]{1,0:T(8,128)}) %all-reduce.6.cloned.1.call-update) | async-done | bytes 131088 | tf_op jit(solution)/shard_map/psum | solution.py:99
  509.4 225.2 %reduce-scatter.2.cloned.1.call-done = f32[256,64]{0,1:T(8,128)} async-done(((f32[8192,64]{0,1:T(8,128)}), f32[256,64]{0,1:T(8,128)}) %reduce-scatter.2.cloned.1.call-update) | async-done | bytes 65552 | tf_op jit(solution)/shard_map/reduce_scatter | solution.py:90
  734.5 0.9 copy.61
  735.4 1.6 copy.62
  (21 shorter events, 0.1 us)
Async XLA Ops:
  8.0 221.7 %copy-start = (bf16[48,8192]{1,0:T(8,128)(2,1)S(1)}, bf16[48,8192]{1,0:T(8,128)(2,1)}, u32[]{:S(2)}) copy-start(bf16[48,8192]{1,0:T(8,128)(2,1)} %param.11) | copy-start | bytes 2359300
  15.1 14.9 %copy-start.7 = (s32[48]{0:T(128)S(1)}, s32[48]{0:T(128)}, u32[]{:S(2)}) copy-start(s32[48]{0:T(128)} %param.17) | copy-start | bytes 580
  15.1 14.9 %copy-start.4 = (bf16[192,512]{1,0:T(8,128)(2,1)S(1)}, bf16[192,512]{1,0:T(8,128)(2,1)}, u32[]{:S(2)}) copy-start(bf16[192,512]{1,0:T(8,128)(2,1)} %param.19) | copy-start | bytes 589828
  15.1 207.2 %copy-start.6 = (f32[48]{0:T(128)S(1)}, f32[48]{0:T(128)}, u32[]{:S(2)}) copy-start(f32[48]{0:T(128)} %param.16) | copy-start | bytes 580
  15.1 207.2 %all-to-all-start = ((bf16[32,256,512]{2,1,0:T(8,128)(2,1)}), bf16[32,256,512]{2,1,0:T(8,128)(2,1)}, u32[]{:S(2)}, u32[]{:S(2)}) async-start(bf16[32,256,512]{2,1,0:T(8,128)(2,1)} %stack.2), calls=%async_computation | async-start | bytes 16777216 | tf_op jit(solution)/shard_map/all_to_all | solution.py:61
  28.6 200.9 %copy-start.5 = (bf16[64,512]{1,0:T(8,128)(2,1)S(1)}, bf16[64,512]{1,0:T(8,128)(2,1)}, u32[]{:S(2)}) copy-start(bf16[64,512]{1,0:T(8,128)(2,1)} %param.15) | copy-start | bytes 196612
  28.6 201.1 %all-gather.2.cloned.1.call-start = ((), (), s32[]{:S(2)}) async-start(), calls=%async_computation.3 | async-start | bytes 1081344 | tf_op jit(solution)/shard_map/all_gather | solution.py:64
  29.3 320.4 %all-reduce.4.cloned.1.call-start = ((), (), s32[]{:S(2)}) async-start(), calls=%async_computation.4 | async-start | bytes 3145728 | tf_op jit(solution)/shard_map/psum | solution.py:80
  229.4 279.9 %all-reduce.6.cloned.1.call-start = ((), (), s32[]{:S(2)}) async-start(), calls=%async_computation.6 | async-start | bytes 262144 | tf_op jit(solution)/shard_map/psum | solution.py:99
  232.5 117.2 %copy-start.1 = (bf16[8192,64]{0,1:T(8,128)(2,1)S(1)}, bf16[8192,64]{0,1:T(8,128)(2,1)}, u32[]{:S(2)}) copy-start(bf16[8192,64]{0,1:T(8,128)(2,1)} %all-gather.2.cloned.1.call-done) | copy-start | bytes 3145732
  232.5 502.0 %reduce-scatter.2.cloned.1.call-start = ((), (), s32[]{:S(2)}) async-start(), calls=%async_computation.5 | async-start | bytes 2162688 | tf_op jit(solution)/shard_map/reduce_scatter | solution.py:90
  237.7 124.0 %copy-start.3 = (bf16[192,512]{1,0:T(8,128)(2,1)S(1)}, bf16[192,512]{1,0:T(8,128)(2,1)}, u32[]{:S(2)}) copy-start(bf16[192,512]{1,0:T(8,128)(2,1)} %param.10) | copy-start | bytes 589828
  352.4 33.6 %all-to-all-start.1 = ((bf16[48,32,256]{2,0,1:T(8,128)(2,1)}), bf16[48,32,256]{2,0,1:T(8,128)(2,1)S(1)}, u32[]{:S(2)}, u32[]{:S(2)}) async-start(bf16[48,32,256]{2,0,1:T(8,128)(2,1)} %bitcast.31), calls=%async_computation.1 | async-start | bytes 1572864 | tf_op jit(solution)/shard_map/all_to_all | solution.py:87
  362.9 374.1 %copy-start.2 = (bf16[192,512]{1,0:T(8,128)(2,1)}, bf16[192,512]{1,0:T(8,128)(2,1)S(1)}, u32[]{:S(2)}) copy-start(bf16[192,512]{1,0:T(8,128)(2,1)S(1)} %scatter_custom_fusion) | copy-start | bytes 589828
Sparse Core Ops, SparseCore 0:
  32.5 124.6 all-gather.1
Sparse Core Ops, SparseCore 1:
  229.5 120.1 all-reduce.3
  354.0 155.3 all-reduce.5
  514.2 220.3 reduce-scatter.1
